TPU v7x, 32 devices: a whole 2x2x4 slice. The times are simulated.
32 devices in a mesh: leaf: 8 (over z, y), tile: 4 (over x, core).
Axes of the slice: x: 2, y: 2, z: 4, core: 2. Of those that a mesh axis runs over, the one named last changes fastest.
Arguments:
- rhs_leaf: float32 [16384, 128], P(('leaf', 'tile')), may hold values from -6 to 6
- rhs_sep: float32 [12288, 128], P(('leaf', 'tile')), may hold values from -6 to 6
- leaf_inv: float32 [16384, 2048], P(('leaf', 'tile')), as said below
- leaf_up: float32 [8, 1536, 2048], P('leaf', None, 'tile'), may hold values from -0.0625 to 0.0625
- sep_inv: float32 [12288, 1536], P(('leaf', 'tile')), as said below
- sep_up: float32 [8, 1536, 1536], P('leaf', None, 'tile'), may hold values from -0.078125 to 0.078125
- live_tiles: int32 [8], replicated, may hold values from 6 to 12, as said below
Outputs:
- leaf_result: float32 [16384, 128], P(('leaf', 'tile'))
- sep_result: float32 [12288, 128], P(('leaf', 'tile'))
Inputs may be any that keep to these rules, and one draw needn't show every extreme that they name: `leaf_inv`: each block of 2048 rows is lower triangular. `sep_inv`: each block of 1536 rows is lower triangular. `live_tiles`: some separator of the lowest level has all 12 tiles live.
All inputs are finite; a program needn't handle non-finite values.
Results may differ from a plain program's by a relative error of at most 0.0003.
Values sent between devices are 32-bit elements; how exact they have to be, the bound alone decides.
A program may use at most 128 MiB of HBM per device.

v0:
```python
import jax
import jax.numpy as jnp
from jax import lax
from jax.sharding import PartitionSpec as P

TILE = 128


HIGHEST = lax.Precision.HIGHEST


def shifted_2(value, axis, steps):
    count = lax.axis_size(axis)
    pairs = [(source, (source + steps) % count) for source in range(count)]
    return lax.ppermute(value, axis, pairs)


def product(first, second):
    return jnp.dot(first, second, precision=HIGHEST, preferred_element_type=jnp.float32)


def product_t(first, second):
    return lax.dot_general(
        first,
        second,
        (((0,), (0,)), ((), ())),
        precision=HIGHEST,
        preferred_element_type=jnp.float32,
    )


def send_up(value, steps):
    return shifted_2(value, "leaf", steps)


def whole_send(value, steps):
    return shifted_2(value, "leaf", steps)


def body(rhs_leaf, rhs_sep, leaf_inv, leaf_up, sep_inv, sep_up, live_tiles):
    leaves = lax.axis_size("leaf")
    depth = leaves.bit_length() - 1
    first_block = leaves // 4 + 1
    leaf_index = lax.axis_index("leaf")
    tile_index = lax.axis_index("tile")
    position = (leaf_index + leaves - first_block) % leaves
    share = rhs_sep.shape[0]
    columns = rhs_sep.shape[1]
    leaf_block = leaf_up[0]
    sep_block = sep_up[0]
    places = jnp.arange(leaves, dtype=jnp.int32)
    my_live = jnp.sum(jnp.where(places == leaf_index, live_tiles, 0))
    row_index = tile_index * share + jnp.arange(share, dtype=jnp.int32)
    mask = (row_index < my_live * TILE).astype(jnp.float32)[:, None]
    zero_share = jnp.zeros((share, columns), jnp.float32)
    leaf_solved = product(leaf_inv, lax.all_gather(rhs_leaf, "tile", axis=0, tiled=True))
    upward = lax.psum_scatter(
        product(leaf_block, leaf_solved), "tile", scatter_dimension=0, tiled=True
    )
    sep_solved = zero_share
    for level in range(1, depth + 1):
        is_owner = (position + 1) % (1 << level) == 1 << level - 1
        if level == 1:
            left_kid = upward
            right_kid = send_up(upward, -1)
        else:
            reach = 1 << level - 2
            right_kid = send_up(upward, -reach)
            left_kid = send_up(upward, reach)
        residue = (rhs_sep - left_kid - right_kid) * mask

        def sep_fold(total, piece, start, is_owner=is_owner):
            return lax.cond(is_owner, lambda: product(sep_inv, piece), lambda: total)

        solved = (
            sep_fold(zero_share, lax.all_gather(residue, "tile", axis=0, tiled=True), jnp.int32(0))
            * mask
        )
        sep_solved = jnp.where(is_owner, solved, sep_solved)
        if level < depth:

            def sep_term(start, count, is_owner=is_owner, solved=solved):
                return lax.cond(
                    is_owner,
                    lambda: product(sep_block, solved),
                    lambda: jnp.zeros((count, columns), jnp.float32),
                )

            upward = lax.psum_scatter(
                sep_term(jnp.int32(0), lax.axis_size("tile") * share),
                "tile",
                scatter_dimension=0,
                tiled=True,
            )
    sep_result = zero_share
    downward = zero_share
    for level in range(depth, 0, -1):
        is_owner = (position + 1) % (1 << level) == 1 << level - 1
        if level == depth:
            residue = sep_solved * mask
        else:
            reach = 1 << level - 1
            is_left = (position + 1) // (1 << level) % 2 == 0
            whole_rows = lax.all_gather(downward, "tile", axis=0, tiled=True)
            above_right = whole_send(whole_rows, -reach)
            above_left = whole_send(whole_rows, reach)
            parent_rows = jnp.where(is_left, above_right, above_left)
            carried = lax.cond(
                is_owner, lambda: product_t(sep_block, parent_rows), lambda: zero_share
            )
            residue = (sep_solved - carried) * mask

        def sep_back(start, count, is_owner=is_owner, residue=residue):
            return lax.cond(
                is_owner,
                lambda: product_t(sep_inv, residue),
                lambda: jnp.zeros((count, columns), jnp.float32),
            )

        result = (
            lax.psum_scatter(
                sep_back(jnp.int32(0), lax.axis_size("tile") * share),
                "tile",
                scatter_dimension=0,
                tiled=True,
            )
            * mask
        )
        sep_result = jnp.where(is_owner, result, sep_result)
        downward = result
    is_odd = position % 2 == 1
    whole_rows = lax.all_gather(downward, "tile", axis=0, tiled=True)
    shifted = whole_send(whole_rows, 1)
    parent_rows = jnp.where(is_odd, shifted, whole_rows)
    carried = product_t(leaf_block, parent_rows)
    leaf_residue = leaf_solved - carried
    leaf_result = lax.psum_scatter(
        product_t(leaf_inv, leaf_residue), "tile", scatter_dimension=0, tiled=True
    )
    return (leaf_result, sep_result)


def solution(mesh):
    return jax.shard_map(
        body,
        mesh=mesh,
        in_specs=(
            P(("leaf", "tile"), None),
            P(("leaf", "tile"), None),
            P(("leaf", "tile"), None),
            P("leaf", None, "tile"),
            P(("leaf", "tile"), None),
            P("leaf", None, "tile"),
            P(),
        ),
        out_specs=(P(("leaf", "tile"), None), P(("leaf", "tile"), None)),
        check_vma=False,
    )
```

profile of v0, /device:TPU:0, one launch (start us, length us, event | category | flops | bytes accessed | tf_op | source)
XLA Modules:
  0.0 472.7 jit_solution(13901635100075003201)
XLA Ops:
  8.0 21.1 %all-gather.2.cloned.1.call-done = f32[2048,128]{1,0:T(8,128)} async-done(((f32[512,128]{1,0:T(8,128)}), f32[2048,128]{1,0:T(8,128)}) %all-gather.2.cloned.1.call-update) | async-done | bytes 1048592 | tf_op jit(solution)/shard_map/all_gather | solution.py:56
  29.0 5.5 %fusion.28 = f32[512,128]{1,0:T(8,128)S(1)} fusion(f32[512,2048]{1,0:T(8,128)} %param.29, f32[2048,128]{1,0:T(8,128)} %all-gather.2.cloned.1.call-done), kind=kOutput, calls=%fused_computation.42 | convolution fusion | flops 1610612736 | bytes 5505024 | tf_op jit(solution)/shard_map/dot_general | solution.py:19
  39.9 23.2 %reduce-scatter.8.cloned.1.call-done = f32[384,128]{0,1:T(8,128)} async-done(((f32[1536,128]{0,1:T(8,128)}), f32[384,128]{0,1:T(8,128)}) %reduce-scatter.8.cloned.1.call-update) | async-done | bytes 196624 | tf_op jit(solution)/shard_map/reduce_scatter | solution.py:57
  72.7 7.7 %all_gather.22 = f32[1536,128]{0,1:T(8,128)S(1)} all-gather(f32[384,128]{0,1:T(8,128)S(1)} %subtract_multiply_fusion.6), channel_id=1, replica_groups=mesh['leaf'=8,'tile'=4] {'tile'}, dimensions={0}, use_global_device_ids=true | all-gather | bytes 983040 | tf_op jit(solution)/shard_map/all_gather | solution.py:76
  84.4 32.8 %reduce-scatter.10.cloned.1.call-done = f32[384,128]{0,1:T(8,128)} async-done(((f32[1536,128]{0,1:T(8,128)}), f32[384,128]{0,1:T(8,128)}) %reduce-scatter.10.cloned.1.call-update) | async-done | bytes 196624 | tf_op jit(solution)/shard_map/reduce_scatter | solution.py:89
  125.9 4.9 %collective-permute-done.1 = f32[384,128]{0,1:T(8,128)} collective-permute-done((f32[384,128]{0,1:T(8,128)}, f32[384,128]{0,1:T(8,128)}, u32[]{:S(2)}, u32[]{:S(2)}) %collective-permute-start.1) | collective-permute-done | bytes 196640 | tf_op jit(solution)/shard_map/ppermute | solution.py:15
  131.9 7.7 %all_gather.23 = f32[1536,128]{0,1:T(8,128)S(1)} all-gather(f32[384,128]{0,1:T(8,128)S(1)} %subtract_multiply_fusion.5), channel_id=1, replica_groups=mesh['leaf'=8,'tile'=4] {'tile'}, dimensions={0}, use_global_device_ids=true | all-gather | bytes 983040 | tf_op jit(solution)/shard_map/all_gather | solution.py:76
  152.1 20.6 %reduce-scatter.12.cloned.1.call-done = f32[384,128]{0,1:T(8,128)} async-done(((f32[1536,128]{0,1:T(8,128)}), f32[384,128]{0,1:T(8,128)}) %reduce-scatter.12.cloned.1.call-update) | async-done | bytes 196624 | tf_op jit(solution)/shard_map/reduce_scatter | solution.py:89
  176.0 5.6 %collective-permute-done.4 = f32[384,128]{0,1:T(8,128)} collective-permute-done((f32[384,128]{0,1:T(8,128)}, f32[384,128]{0,1:T(8,128)}, u32[]{:S(2)}, u32[]{:S(2)}) %collective-permute-start.4) | collective-permute-done | bytes 196640 | tf_op jit(solution)/shard_map/ppermute | solution.py:15
  186.8 7.7 %all_gather.24 = f32[1536,128]{0,1:T(8,128)S(1)} all-gather(f32[384,128]{0,1:T(8,128)S(1)} %subtract_multiply_fusion.4), channel_id=1, replica_groups=mesh['leaf'=8,'tile'=4] {'tile'}, dimensions={0}, use_global_device_ids=true | all-gather | bytes 983040 | tf_op jit(solution)/shard_map/all_gather | solution.py:76
  196.5 29.3 %reduce-scatter.14.cloned.1.call-done = f32[384,128]{0,1:T(8,128)} async-done(((f32[1536,128]{0,1:T(8,128)}), f32[384,128]{0,1:T(8,128)}) %reduce-scatter.14.cloned.1.call-update) | async-done | bytes 196624 | tf_op jit(solution)/shard_map/reduce_scatter | solution.py:121
  226.7 8.6 %all_gather.25 = f32[1536,128]{0,1:T(8,128)} all-gather(f32[384,128]{0,1:T(8,128)S(1)} %broadcast_multiply_fusion.1), channel_id=1, replica_groups=mesh['leaf'=8,'tile'=4] {'tile'}, dimensions={0}, use_global_device_ids=true | all-gather | bytes 983040 | tf_op jit(solution)/shard_map/all_gather | solution.py:104
  239.2 18.7 %collective-permute-done.6 = f32[1536,128]{0,1:T(8,128)} collective-permute-done((f32[1536,128]{0,1:T(8,128)}, f32[1536,128]{0,1:T(8,128)}, u32[]{:S(2)}, u32[]{:S(2)}) %collective-permute-start.6) | collective-permute-done | bytes 786464 | tf_op jit(solution)/shard_map/ppermute | solution.py:15
  257.9 15.7 %collective-permute-done.5 = f32[1536,128]{0,1:T(8,128)} collective-permute-done((f32[1536,128]{0,1:T(8,128)}, f32[1536,128]{0,1:T(8,128)}, u32[]{:S(2)}, u32[]{:S(2)}) %collective-permute-start.5) | collective-permute-done | bytes 786464 | tf_op jit(solution)/shard_map/ppermute | solution.py:15
  273.5 8.5 %conditional.16 = (f32[384,128]{0,1:T(8,128)S(1)}) conditional(s32[]{:T(128)} %convert_element_type.25, () %tuple.91, (pred[]{:T(512)}, f32[1536,128]{0,1:T(8,128)}, f32[1536,128]{0,1:T(8,128)}, f32[1536,384]{1,0:T(8,128)}, pred[]{:T(512)}, /*index=5*/s32[]{:T(128)}, pred[]{:T(512)}, s32[]{:T(128)}, s32[]{:T(128)}) %tuple.155), branch_computations={%region_17.18_spmd, %region_18.19_spmd} | conditional | flops 906166272 | bytes 7274672 | solution.py:108
  282.8 7.8 %conditional.17 = (f32[1536,128]{0,1:T(8,128)}) conditional(s32[]{:T(128)} %convert_element_type.25, () %tuple.90, (f32[384,1536]{1,0:T(8,128)}, f32[384,128]{0,1:T(8,128)S(1)}, f32[384,128]{0,1:T(8,128)S(1)}, f32[384,128]{0,1:T(8,128)}) %tuple.157), branch_computations={%region_19.20_spmd, %region_20.21_spmd} | conditional | flops 906067968 | bytes 4915208 | solution.py:114
  290.7 20.7 %reduce-scatter.16.cloned.1.call-done = f32[384,128]{0,1:T(8,128)} async-done(((f32[1536,128]{0,1:T(8,128)}), f32[384,128]{0,1:T(8,128)}) %reduce-scatter.16.cloned.1.call-update) | async-done | bytes 196624 | tf_op jit(solution)/shard_map/reduce_scatter | solution.py:121
  312.3 8.7 %all_gather.26 = f32[1536,128]{0,1:T(8,128)} all-gather(f32[384,128]{0,1:T(8,128)S(1)} %broadcast_multiply_fusion), channel_id=1, replica_groups=mesh['leaf'=8,'tile'=4] {'tile'}, dimensions={0}, use_global_device_ids=true | all-gather | bytes 983040 | tf_op jit(solution)/shard_map/all_gather | solution.py:104
  325.7 31.2 %collective-permute-done.8 = f32[1536,128]{0,1:T(8,128)} collective-permute-done((f32[1536,128]{0,1:T(8,128)}, f32[1536,128]{0,1:T(8,128)}, u32[]{:S(2)}, u32[]{:S(2)}) %collective-permute-start.8) | collective-permute-done | bytes 786464 | tf_op jit(solution)/shard_map/ppermute | solution.py:15
  360.9 36.9 %reduce-scatter.18.cloned.1.call-done = f32[384,128]{0,1:T(8,128)} async-done(((f32[1536,128]{0,1:T(8,128)}), f32[384,128]{0,1:T(8,128)}) %reduce-scatter.18.cloned.1.call-update) | async-done | bytes 196624 | tf_op jit(solution)/shard_map/reduce_scatter | solution.py:121
  399.6 8.6 %all_gather.27 = f32[1536,128]{0,1:T(8,128)} all-gather(f32[384,128]{0,1:T(8,128)S(1)} %get-tuple-element.306), channel_id=1, replica_groups=mesh['leaf'=8,'tile'=4] {'tile'}, dimensions={0}, use_global_device_ids=true | all-gather | bytes 983040 | tf_op jit(solution)/shard_map/all_gather | solution.py:132
  410.0 21.3 %collective-permute-done.9 = f32[1536,128]{0,1:T(8,128)} collective-permute-done((f32[1536,128]{0,1:T(8,128)}, f32[1536,128]{0,1:T(8,128)}, u32[]{:S(2)}, u32[]{:S(2)}) %collective-permute-start.9) | collective-permute-done | bytes 786464 | tf_op jit(solution)/shard_map/ppermute | solution.py:15
  431.3 6.2 %fusion.16 = f32[512,128]{1,0:T(8,128)S(1)} fusion(f32[512,128]{1,0:T(8,128)S(1)} %copy-done.3, f32[1,1536,512]{2,1,0:T(8,128)S(1)} %copy-done, f32[1536,128]{0,1:T(8,128)} %collective-permute-done.9, f32[1536,128]{0,1:T(8,128)} %all_gather.27, pred[]{:T(512)S(6)} %eq.44), kind=kOutput, calls=%fused_computation.20 | convolution fusion | flops 1208221696 | bytes 5242881 | tf_op jit(solution)/shard_map/dot_general | solution.py:23
  441.7 21.9 %reduce-scatter.20.cloned.1.call-done = f32[512,128]{0,1:T(8,128)} async-done(((f32[2048,128]{0,1:T(8,128)}), f32[512,128]{0,1:T(8,128)}) %reduce-scatter.20.cloned.1.call-update) | async-done | bytes 262160 | tf_op jit(solution)/shard_map/reduce_scatter | solution.py:137
  (90 shorter events, 104.8 us)
Async XLA Ops:
  7.2 28.1 %copy-start = (f32[1,1536,512]{2,1,0:T(8,128)S(1)}, f32[1,1536,512]{2,1,0:T(8,128)}, u32[]{:S(2)}) copy-start(f32[1,1536,512]{2,1,0:T(8,128)} %param.30) | copy-start | bytes 9437188
  7.2 21.8 %all-gather.2.cloned.1.call-start = ((), (), s32[]{:S(2)}) async-start(), calls=%async_computation.7 | async-start | bytes 1310720 | tf_op jit(solution)/shard_map/all_gather | solution.py:56
  7.9 55.1 %reduce-scatter.8.cloned.1.call-start = ((), (), s32[]{:S(2)}) async-start(), calls=%async_computation.8 | async-start | bytes 983040 | tf_op jit(solution)/shard_map/reduce_scatter | solution.py:57
  35.2 4.5 copy-start.7
  35.2 32.0 %copy-start.8 = (s32[8]{0:T(128)S(1)}, s32[8]{0:T(128)}, u32[]{:S(2)}) copy-start(s32[8]{0:T(128)} %param.33) | copy-start | bytes 100
  39.6 77.6 %reduce-scatter.10.cloned.1.call-start = ((), (), s32[]{:S(2)}) async-start(), calls=%async_computation.9 | async-start | bytes 983040 | tf_op jit(solution)/shard_map/reduce_scatter | solution.py:89
  63.1 8.7 %collective-permute-start = (f32[384,128]{0,1:T(8,128)}, f32[384,128]{0,1:T(8,128)S(1)}, u32[]{:S(2)}, u32[]{:S(2)}) collective-permute-start(f32[384,128]{0,1:T(8,128)} %reduce-scatter.8.cloned.1.call-done), channel_id=1, source_target_pairs={{0,28},{4,0},{8,4},{12,8},{16,12},{20,16},{24,20},{28,24},{1,29},{... | collective-permute-start | bytes 589832 | tf_op jit(solution)/shard_map/ppermute | solution.py:15
  84.4 88.3 %reduce-scatter.12.cloned.1.call-start = ((), (), s32[]{:S(2)}) async-start(), calls=%async_computation.10 | async-start | bytes 983040 | tf_op jit(solution)/shard_map/reduce_scatter | solution.py:89
  117.2 8.7 %collective-permute-start.2 = (f32[384,128]{0,1:T(8,128)}, f32[384,128]{0,1:T(8,128)}, u32[]{:S(2)}, u32[]{:S(2)}) collective-permute-start(f32[384,128]{0,1:T(8,128)} %reduce-scatter.10.cloned.1.call-done), channel_id=1, source_target_pairs={{0,28},{4,0},{8,4},{12,8},{16,12},{20,16},{24,20},{28,24},{1,29},{... | collective-permute-start | bytes 589832 | tf_op jit(solution)/shard_map/ppermute | solution.py:15
  121.5 9.4 %collective-permute-start.1 = (f32[384,128]{0,1:T(8,128)}, f32[384,128]{0,1:T(8,128)}, u32[]{:S(2)}, u32[]{:S(2)}) collective-permute-start(f32[384,128]{0,1:T(8,128)} %reduce-scatter.10.cloned.1.call-done), channel_id=1, source_target_pairs={{0,4},{4,8},{8,12},{12,16},{16,20},{20,24},{24,28},{28,0},{1,5},{5... | collective-permute-start | bytes 589832 | tf_op jit(solution)/shard_map/ppermute | solution.py:15
  152.0 73.8 %reduce-scatter.14.cloned.1.call-start = ((), (), s32[]{:S(2)}) async-start(), calls=%async_computation.11 | async-start | bytes 983040 | tf_op jit(solution)/shard_map/reduce_scatter | solution.py:121
  172.7 8.9 %collective-permute-start.4 = (f32[384,128]{0,1:T(8,128)}, f32[384,128]{0,1:T(8,128)}, u32[]{:S(2)}, u32[]{:S(2)}) collective-permute-start(f32[384,128]{0,1:T(8,128)} %reduce-scatter.12.cloned.1.call-done), channel_id=1, source_target_pairs={{0,24},{4,28},{8,0},{12,4},{16,8},{20,12},{24,16},{28,20},{1,25},{... | collective-permute-start | bytes 589832 | tf_op jit(solution)/shard_map/ppermute | solution.py:15
  176.0 9.7 %collective-permute-start.3 = (f32[384,128]{0,1:T(8,128)}, f32[384,128]{0,1:T(8,128)}, u32[]{:S(2)}, u32[]{:S(2)}) collective-permute-start(f32[384,128]{0,1:T(8,128)} %reduce-scatter.12.cloned.1.call-done), channel_id=1, source_target_pairs={{0,8},{4,12},{8,16},{12,20},{16,24},{20,28},{24,0},{28,4},{1,9},{5... | collective-permute-start | bytes 589832 | tf_op jit(solution)/shard_map/ppermute | solution.py:15
  196.4 114.9 %reduce-scatter.16.cloned.1.call-start = ((), (), s32[]{:S(2)}) async-start(), calls=%async_computation.12 | async-start | bytes 983040 | tf_op jit(solution)/shard_map/reduce_scatter | solution.py:121
  235.4 22.5 %collective-permute-start.6 = (f32[1536,128]{0,1:T(8,128)}, f32[1536,128]{0,1:T(8,128)}, u32[]{:S(2)}, u32[]{:S(2)}) collective-permute-start(f32[1536,128]{0,1:T(8,128)} %all_gather.25), channel_id=1, source_target_pairs={{0,8},{4,12},{8,16},{12,20},{16,24},{20,28},{24,0},{28,4},{1,9},{5... | collective-permute-start | bytes 2359304 | tf_op jit(solution)/shard_map/ppermute | solution.py:15
  236.8 36.7 %collective-permute-start.5 = (f32[1536,128]{0,1:T(8,128)}, f32[1536,128]{0,1:T(8,128)}, u32[]{:S(2)}, u32[]{:S(2)}) collective-permute-start(f32[1536,128]{0,1:T(8,128)} %all_gather.25), channel_id=1, source_target_pairs={{0,24},{4,28},{8,0},{12,4},{16,8},{20,12},{24,16},{28,20},{1,25},{... | collective-permute-start | bytes 2359304 | tf_op jit(solution)/shard_map/ppermute | solution.py:15
  290.6 107.1 %reduce-scatter.18.cloned.1.call-start = ((), (), s32[]{:S(2)}) async-start(), calls=%async_computation.13 | async-start | bytes 983040 | tf_op jit(solution)/shard_map/reduce_scatter | solution.py:121
  321.0 36.0 %collective-permute-start.8 = (f32[1536,128]{0,1:T(8,128)}, f32[1536,128]{0,1:T(8,128)}, u32[]{:S(2)}, u32[]{:S(2)}) collective-permute-start(f32[1536,128]{0,1:T(8,128)} %all_gather.26), channel_id=1, source_target_pairs={{0,4},{4,8},{8,12},{12,16},{16,20},{20,24},{24,28},{28,0},{1,5},{5... | collective-permute-start | bytes 2359304 | tf_op jit(solution)/shard_map/ppermute | solution.py:15
  322.5 36.7 %collective-permute-start.7 = (f32[1536,128]{0,1:T(8,128)}, f32[1536,128]{0,1:T(8,128)}, u32[]{:S(2)}, u32[]{:S(2)}) collective-permute-start(f32[1536,128]{0,1:T(8,128)} %all_gather.26), channel_id=1, source_target_pairs={{0,28},{4,0},{8,4},{12,8},{16,12},{20,16},{24,20},{28,24},{1,29},{... | collective-permute-start | bytes 2359304 | tf_op jit(solution)/shard_map/ppermute | solution.py:15
  360.8 70.5 %copy-start.3 = (f32[512,128]{1,0:T(8,128)S(1)}, f32[512,128]{1,0:T(8,128)}, u32[]{:S(2)}) copy-start(f32[512,128]{1,0:T(8,128)} %copy-done.2) | copy-start | bytes 786436
  360.8 102.8 %reduce-scatter.20.cloned.1.call-start = ((), (), s32[]{:S(2)}) async-start(), calls=%async_computation.14 | async-start | bytes 1310720 | tf_op jit(solution)/shard_map/reduce_scatter | solution.py:137
  408.3 23.0 %collective-permute-start.9 = (f32[1536,128]{0,1:T(8,128)}, f32[1536,128]{0,1:T(8,128)}, u32[]{:S(2)}, u32[]{:S(2)}) collective-permute-start(f32[1536,128]{0,1:T(8,128)} %all_gather.27), channel_id=1, source_target_pairs={{0,4},{4,8},{8,12},{12,16},{16,20},{20,24},{24,28},{28,0},{1,5},{5... | collective-permute-start | bytes 2359304 | tf_op jit(solution)/shard_map/ppermute | solution.py:15
  410.0 27.5 %copy-start.1 = (f32[512,2048]{1,0:T(8,128)S(1)}, f32[512,2048]{1,0:T(8,128)}, u32[]{:S(2)}) copy-start(f32[512,2048]{1,0:T(8,128)} %param.29) | copy-start | bytes 12582916
  437.5 3.4 copy-start.6
  (3 other events, 2.1 us)
Sparse Core Ops, SparseCore 0:
  9.6 19.4 all-gather.1
  39.8 23.2 reduce-scatter.7
  84.5 32.6 reduce-scatter.9
  152.1 20.5 reduce-scatter.11
  196.6 29.1 reduce-scatter.13
  290.8 20.5 reduce-scatter.15
  361.0 36.7 reduce-scatter.17
  441.0 22.5 reduce-scatter.19
where the time goes:
time: 481 us; the launch traced here: 473 us
  waiting for transfers between devices  319 us (66%)
  blocking collectives  48.9 us (10%)
  matrix products  36.2 us (8%)
  starting transfers between devices  22.4 us (5%)
  local copies, waits for them, and re-layouts  21 us (4%)
  between operations  15.4 us (3%)
  other arithmetic  9.77 us (2%)
    ppermute x10, waiting for transfers between devices, shifted_2(): return lax.ppermute(value, axis, pairs)  111 us
    reduce_scatter x3, waiting for transfers between devices, body(): lax.psum_scatter(sep_back(jnp.int32(0), lax.axis_size('tile') * share), '...  86.9 us
    reduce_scatter x2, waiting for transfers between devices, body(): lax.psum_scatter(sep_term(jnp.int32(0), lax.axis_size('tile') * share), '...  53.4 us
    all_gather x3, blocking collectives, body(): whole_rows = lax.all_gather(downward, 'tile', axis=0, tiled=True)  25.9 us
    reduce_scatter x1, waiting for transfers between devices, body(): lax.psum_scatter(product(leaf_block, leaf_solved), 'tile', scatter_dimens...  23.2 us
    all_gather x3, blocking collectives, body(): lax.all_gather(residue, 'tile', axis=0, tiled=True)  23 us
    ppermute x10, starting transfers between devices, shifted_2(): return lax.ppermute(value, axis, pairs)  22.1 us
    reduce_scatter x1, waiting for transfers between devices, body(): lax.psum_scatter(product_t(leaf_inv, leaf_residue), 'tile', scatter_dimen...  21.9 us
  transfers between devices with their start and end apart: 18, of which 18 were waited for; matrix products, arithmetic and copies ran while one was open for 0% of the time, Pallas kernels for 0%

commit v1 on v0

v1 whole, which is shorter than its diff:
```python
import functools
import jax
import jax.numpy as jnp
from jax import lax
from jax.experimental import pallas as pl
from jax.experimental.pallas import tpu as pltpu
from jax.sharding import PartitionSpec as P

TILE = 128
PIECES = 2
MESH = pl.DeviceIdType.MESH
F32 = jnp.float32
BF16 = jnp.bfloat16

LEAF_GATHER, LEAF_SUM, SEP_GATHER, SEP_SUM = 0, 3, 6, 9
BACK_GATHER, BACK_SUM, LAST_GATHER, LAST_SUM = 12, 15, 18, 21
KID, ABOVE, LEAF_ABOVE, ABOVE_RIGHT = 24, 26, 27, 28
KINDS = 29


def split(value):
    high = value.astype(BF16)
    return high, (value - high.astype(F32)).astype(BF16)


def times(value, high_ref, low_ref, index, transposed):
    dims = (((1,), (1 if transposed else 0,)), ((), ()))
    rows = value.shape[0]
    high, low = split(value)
    both = jnp.concatenate([high, low], axis=0)
    first = lax.dot_general(both, high_ref[index], dims, preferred_element_type=F32)
    second = lax.dot_general(high, low_ref[index], dims, preferred_element_type=F32)
    return first[:rows] + first[rows:] + second


def kernel(
    leaves,
    live_ref,
    rhs_leaf,
    rhs_sep,
    leaf_inv,
    leaf_up,
    sep_inv,
    sep_up,
    leaf_out,
    sep_out,
    rhs_l,
    rhs_s,
    li,
    lu,
    si,
    su,
    li_h,
    li_l,
    lu_h,
    lu_l,
    si_h,
    si_l,
    su_h,
    su_l,
    gather_l,
    gather_s,
    gather_b,
    gather_c,
    part_l,
    part_s,
    part_b,
    part_c,
    one_l,
    one_s,
    one_b,
    one_c,
    two_l,
    two_s,
    two_b,
    two_c,
    kid,
    solved_l,
    solved_s,
    acc_s,
    acc_l,
    load_sem,
    send_sem,
    recv_sem,
):
    depth = leaves.bit_length() - 1
    first_block = leaves // 4 + 1
    leaf = lax.axis_index("leaf")
    t = lax.axis_index("tile")
    core = t % 2
    half = t // 2
    sib = t + 1 - 2 * core
    acr = (t + 2) % 4
    far = (sib + 2) % 4
    pos = (leaf + leaves - first_block) % leaves
    ahead = pos + 1
    share = rhs_s.shape[0]
    cols = rhs_s.shape[1]
    rows = cols // PIECES

    def block_of(place):
        return (place + leaves + first_block) % leaves

    level_one = ahead % 2 == 1
    has_sep = pos < leaves - 1
    is_top = ahead == leaves // 2
    not_top = jnp.logical_and(has_sep, ahead != leaves // 2)
    has_kids = jnp.logical_and(has_sep, ahead % 2 == 0)
    parent = pos * 0
    side = pos * 0
    reach = pos * 0
    for level in range(1, depth + 1):
        own = (ahead % (1 << level) == (1 << (level - 1))).astype(jnp.int32)
        odd = (ahead // (1 << level)) % 2
        step = 1 << (level - 1)
        parent = parent + own * (pos + step - 2 * step * odd)
        side = side + own * odd
        reach = reach + own * (step // 2)
    up_block = block_of(parent)
    left_block = block_of(pos - reach)
    right_block = block_of(pos + reach)
    pair_block = block_of(pos + 1 - 2 * (pos % 2))

    def loads(kind, source, target, by_column):
        out = []
        for q in range(4):
            if by_column:
                width = target.shape[2]
                view = source.at[:, pl.ds(q * width, width)]
            else:
                height = target.shape[1]
                view = source.at[pl.ds(q * height, height), :]
            out.append(pltpu.make_async_copy(view, target.at[q], load_sem.at[kind, q]))
        return out

    load_rl = pltpu.make_async_copy(rhs_leaf, rhs_l, load_sem.at[4, 0])
    load_rs = pltpu.make_async_copy(rhs_sep, rhs_s, load_sem.at[4, 1])
    load_li = loads(0, leaf_inv, li, True)
    load_lu = loads(1, leaf_up, lu, False)
    load_si = loads(2, sep_inv, si, True)
    load_su = loads(3, sep_up, su, False)
    load_rl.start()
    for copy in load_li + load_lu:
        copy.start()
    load_rs.start()
    for copy in load_si + load_su:
        copy.start()

    barrier = pltpu.get_barrier_semaphore()

    def greet(block, tile):
        pl.semaphore_signal(barrier, inc=1, device_id=(block, tile), device_id_type=MESH)

    greet(leaf, sib)
    greet(leaf, acr)
    greet(pair_block, t)

    @pl.when(not_top)
    def _():
        greet(up_block, t)

    @pl.when(has_kids)
    def _():
        greet(left_block, t)
        greet(right_block, t)

    def split_weights(copies, source, high, low):
        for q in range(4):
            copies[q].wait()
            height = source.shape[1]

            def body(i, carry, q=q):
                at = pl.ds(pl.multiple_of(i * 64, 64), 64)
                h, l = split(source[q, at, :])
                high[q, at, :] = h
                low[q, at, :] = l
                return carry

            lax.fori_loop(0, height // 64, body, 0)

    load_rl.wait()
    gather_l[t] = rhs_l[...].T

    pl.semaphore_wait(
        barrier, 3 + not_top.astype(jnp.int32) + 2 * has_kids.astype(jnp.int32)
    )

    pending = []

    def when(cond, run):
        if cond is None:
            run()
        else:
            pl.when(cond)(run)

    def piece(ref, q, p):
        at = pl.ds(p * rows, rows)
        return lambda: ref.at[at] if q is None else ref.at[q, at]

    def remote(kind, p, source, target, block, tile):
        return pltpu.make_async_remote_copy(
            src_ref=source(),
            dst_ref=target(),
            send_sem=send_sem.at[kind, p],
            recv_sem=recv_sem.at[kind, p],
            device_id=(block, tile),
            device_id_type=MESH,
        )

    def send(kind, p, source, target, block, tile, cond, outer, slot=None):
        def make():
            copy = pltpu.make_async_remote_copy(
                src_ref=source(),
                dst_ref=target(),
                send_sem=send_sem.at[kind, p],
                recv_sem=recv_sem.at[kind if slot is None else slot, p],
                device_id=(block, tile),
                device_id_type=MESH,
            )
            return copy

        when(cond, lambda: make().start())
        pending.append((outer, cond, lambda: make().wait_send()))

    def arrive(kind, p, target):
        remote(kind, p, target, target, leaf, sib).wait_recv()

    def at(p):
        return pl.ds(p * rows, rows)

    low_core, high_core = core == 0, core == 1
    low_half, high_half = half == 0, half == 1

    def gather_send(kind, ref, p, triangle, outer):
        mine = piece(ref, t, p)
        send(kind + 1, p, mine, mine, leaf, acr, low_half if triangle else None, outer)
        send(kind, p, mine, mine, leaf, sib, low_core if triangle else None, outer)

    def gather_use(kind, ref, acc, high, low, triangle, outer, transposed, between=None):
        def add(q, p):
            acc[at(p), :] += times(ref[q, at(p), :], high, low, q, transposed)

        for p in range(PIECES):
            acc[at(p), :] = times(ref[t, at(p), :], high, low, t, transposed)
        if between is not None:
            between()
        for p in range(PIECES):

            def from_sib(p=p):
                arrive(kind, p, piece(ref, sib, p))
                add(sib, p)

            when(high_core if triangle else None, from_sib)
        for p in range(PIECES):

            def from_acr(p=p):
                got = piece(ref, acr, p)
                arrive(kind + 1, p, got)
                remote(kind + 2, p, got, got, leaf, sib).start()
                add(acr, p)

            when(high_half if triangle else None, from_acr)

            def sent(p=p):
                got = piece(ref, acr, p)
                remote(kind + 2, p, got, got, leaf, sib).wait_send()

            pending.append((outer, high_half if triangle else None, sent))
        for p in range(PIECES):

            def from_far(p=p):
                arrive(kind + 2, p, piece(ref, far, p))
                add(far, p)

            when(high_half if triangle else None, from_far)

    def sum_scatter(kind, value, part, one, two, high, low, triangle, outer, transposed, then, between=None):
        over = high_half if triangle else None

        def work(q, p):
            part[q, at(p), :] = times(value[at(p), :], high, low, q, transposed)

        for p in range(PIECES):
            when(over, lambda p=p: work(far, p))
            send(kind, p, piece(part, far, p), piece(one, 0, p), leaf, sib, over, outer)
        for p in range(PIECES):
            when(over, lambda p=p: work(acr, p))
        for p in range(PIECES):

            def pass_on(p=p):
                arrive(kind, p, piece(one, 0, p))
                part[acr, at(p), :] += one[0, at(p), :]

            when(over, pass_on)
            send(kind + 1, p, piece(part, acr, p), piece(two, None, p), leaf, acr, over, outer)
        for p in range(PIECES):
            when(high_core if triangle else None, lambda p=p: work(sib, p))
            send(
                kind + 2,
                p,
                piece(part, sib, p),
                piece(one, 1, p),
                leaf,
                sib,
                high_core if triangle else None,
                outer,
            )
        for p in range(PIECES):
            work(t, p)
        if between is not None:
            between()
        for p in range(PIECES):

            def from_sib(p=p):
                arrive(kind + 2, p, piece(one, 1, p))
                part[t, at(p), :] += one[1, at(p), :]

            when(low_core if triangle else None, from_sib)
        for p in range(PIECES):

            def from_acr(p=p):
                arrive(kind + 1, p, piece(two, None, p))
                part[t, at(p), :] += two[at(p), :]

            when(low_half if triangle else None, from_acr)
            then(p)

    for p in range(PIECES):
        gather_send(LEAF_GATHER, gather_l, p, True, None)
    split_weights(load_li, li, li_h, li_l)
    gather_use(
        LEAF_GATHER,
        gather_l,
        solved_l,
        li_h,
        li_l,
        True,
        None,
        True,
        lambda: split_weights(load_lu, lu, lu_h, lu_l),
    )
    is_odd = pos % 2 == 1
    is_even = pos % 2 == 0

    def leaf_done(p):
        @pl.when(is_even)
        def _():
            kid[0, at(p), :] = part_l[t, at(p), :]

        send(KID, p, piece(part_l, t, p), piece(kid, 1, p), pair_block, t, is_odd, None, KID + 1)

    def prepare():
        split_weights(load_si, si, si_h, si_l)
        split_weights(load_su, su, su_h, su_l)
        load_rs.wait()

    sum_scatter(
        LEAF_SUM, solved_l, part_l, one_l, two_l, lu_h, lu_l, False, None, True, leaf_done, prepare
    )

    live = live_ref[leaf]
    index = lax.broadcasted_iota(jnp.int32, (1, share), 1) + t * share
    mask = jnp.where(index < live * TILE, 1.0, 0.0).astype(F32)

    @pl.when(has_sep)
    def _():
        acc_s[...] = rhs_s[...].T
        for p in range(PIECES):

            @pl.when(has_kids)
            def _():
                arrive(KID, p, piece(kid, 0, p))

            arrive(KID + 1, p, piece(kid, 1, p))
            gather_s[t, at(p), :] = (
                acc_s[at(p), :] - kid[0, at(p), :] - kid[1, at(p), :]
            ) * mask
            gather_send(SEP_GATHER, gather_s, p, True, has_sep)
        gather_use(SEP_GATHER, gather_s, solved_s, si_h, si_l, True, has_sep, True)
        solved_s[...] = solved_s[...] * mask

        @pl.when(not_top)
        def _():
            def sep_done(p):
                def make(wait):
                    copy = pltpu.make_async_remote_copy(
                        src_ref=piece(part_s, t, p)(),
                        dst_ref=kid.at[side, at(p)],
                        send_sem=send_sem.at[ABOVE_RIGHT, p],
                        recv_sem=recv_sem.at[KID + side, p],
                        device_id=(up_block, t),
                        device_id_type=MESH,
                    )
                    return copy.wait_send() if wait else copy.start()

                make(False)
                pending.append((not_top, None, lambda p=p: make(True)))

            sum_scatter(
                SEP_SUM, solved_s, part_s, one_s, two_s, su_h, su_l, False, not_top, True, sep_done
            )
            for p in range(PIECES):
                arrive(ABOVE, p, piece(gather_b, t, p))
                gather_send(BACK_GATHER, gather_b, p, False, not_top)
            gather_use(BACK_GATHER, gather_b, acc_s, su_h, su_l, False, not_top, False)
            solved_s[...] = (solved_s[...] - acc_s[...]) * mask

        def back_done(p):
            part_b[t, at(p), :] = part_b[t, at(p), :] * mask
            mine = piece(part_b, t, p)
            there = piece(gather_b, t, p)
            send(ABOVE, p, mine, there, left_block, t, has_kids, has_sep)
            send(ABOVE_RIGHT + 1, p, mine, there, right_block, t, has_kids, has_sep, ABOVE)

            @pl.when(level_one)
            def _():
                gather_c[t, at(p), :] = part_b[t, at(p), :]

            here = piece(gather_c, t, p)
            send(LEAF_ABOVE, p, here, here, pair_block, t, level_one, has_sep)

        sum_scatter(
            BACK_SUM, solved_s, part_b, one_b, two_b, si_h, si_l, True, has_sep, False, back_done
        )

    for p in range(PIECES):

        @pl.when(is_odd)
        def _():
            arrive(LEAF_ABOVE, p, piece(gather_c, t, p))

        gather_send(LAST_GATHER, gather_c, p, False, None)

    @pl.when(has_sep)
    def _():
        sep_out[...] = part_b[t].T

    @pl.when(pos == leaves - 1)
    def _():
        sep_out[...] = jnp.zeros_like(sep_out)

    gather_use(LAST_GATHER, gather_c, acc_l, lu_h, lu_l, False, None, False)
    solved_l[...] = solved_l[...] - acc_l[...]
    sum_scatter(
        LAST_SUM,
        solved_l,
        part_c,
        one_c,
        two_c,
        li_h,
        li_l,
        True,
        None,
        False,
        lambda p: None,
    )
    leaf_out[...] = part_c[t].T
    for outer, cond, wait in pending:
        when(outer, lambda cond=cond, wait=wait: when(cond, wait))


def body(rhs_leaf, rhs_sep, leaf_inv, leaf_up, sep_inv, sep_up, live_tiles):
    leaves = lax.axis_size("leaf")
    tall, cols = rhs_leaf.shape
    share = rhs_sep.shape[0]
    whole = 4 * share
    any_space = pl.BlockSpec(memory_space=pl.ANY)

    def f32(*shape):
        return pltpu.VMEM(shape, F32)

    weights = [(4, tall, tall), (4, share, tall), (4, share, share), (4, share, share)]
    halves = [pltpu.VMEM(shape, BF16) for shape in weights for _ in range(2)]
    scratch = (
        [f32(tall, cols), f32(share, cols)]
        + [f32(*shape) for shape in weights]
        + halves
        + [f32(4, cols, tall)]
        + [f32(4, cols, share)] * 3
        + [f32(4, cols, share)] * 3
        + [f32(4, cols, tall)]
        + [f32(2, cols, share)] * 3
        + [f32(2, cols, tall)]
        + [f32(cols, share)] * 3
        + [f32(cols, tall)]
        + [f32(2, cols, share), f32(cols, tall), f32(cols, share), f32(cols, share), f32(cols, tall)]
        + [
            pltpu.SemaphoreType.DMA((5, 4)),
            pltpu.SemaphoreType.DMA((KINDS + 1, PIECES)),
            pltpu.SemaphoreType.DMA((KINDS + 1, PIECES)),
        ]
    )
    work = 4 * cols * (tall * 4 * tall + whole * tall + 2 * whole * share)
    return tuple(
        pl.pallas_call(
            functools.partial(kernel, leaves),
            out_shape=(
                jax.ShapeDtypeStruct((tall, cols), F32),
                jax.ShapeDtypeStruct((share, cols), F32),
            ),
            in_specs=[pl.BlockSpec(memory_space=pltpu.SMEM)] + [any_space] * 6,
            out_specs=(
                pl.BlockSpec(memory_space=pltpu.VMEM),
                pl.BlockSpec(memory_space=pltpu.VMEM),
            ),
            scratch_shapes=scratch,
            compiler_params=pltpu.CompilerParams(
                collective_id=0, has_side_effects=True, vmem_limit_bytes=56 * 1024 * 1024
            ),
            cost_estimate=pl.CostEstimate(flops=work, bytes_accessed=12 << 20, transcendentals=0),
        )(live_tiles, rhs_leaf, rhs_sep, leaf_inv, leaf_up[0], sep_inv, sep_up[0])
    )


def solution(mesh):
    return jax.shard_map(
        body,
        mesh=mesh,
        in_specs=(
            P(("leaf", "tile"), None),
            P(("leaf", "tile"), None),
            P(("leaf", "tile"), None),
            P("leaf", None, "tile"),
            P(("leaf", "tile"), None),
            P("leaf", None, "tile"),
            P(),
        ),
        out_specs=(P(("leaf", "tile"), None), P(("leaf", "tile"), None)),
        check_vma=False,
    )
```

time: 481 us -> 147 us (0.31); the launches traced: 473 us -> 146 us
  waiting for transfers between devices: 319 us -> 0 us
  Pallas kernels: 0 us -> 142 us
  blocking collectives: 48.9 us -> 0 us
  matrix products: 36.2 us -> 0 us
  starting transfers between devices: 22.4 us -> 0 us
  local copies, waits for them, and re-layouts: 21 us -> 3.29 us
  between operations: 15.4 us -> 0.64 us
  other arithmetic: 9.77 us -> 0 us
    reduce_scatter x7 -> x0, waiting for transfers between devices: 185 us -> none  [the longest x3 86.9 us: body(): lax.psum_scatter(sep_back(jnp.int32(0), lax.axis_size('tile') * share), '...]
    pallas_call x0 -> x1, Pallas kernels: none -> 142 us  [body(): pl.pallas_call(functools.partial(kernel, leaves), out_shape=(jax.ShapeDty...]
    ppermute x10 -> x0, waiting for transfers between devices: 111 us -> none  [shifted_2(): return lax.ppermute(value, axis, pairs)]
    all_gather x6 -> x0, blocking collectives: 48.9 us -> none  [the longest x3 25.9 us: body(): whole_rows = lax.all_gather(downward, 'tile', axis=0, tiled=True)]
    dot_general x7 -> x0, matrix products: 32.2 us -> none  [the longest x4 17.7 us: product_t(): lax.dot_general(first, second, (((0,), (0,)), ((), ())), precision=HIGHES...]
    ppermute x10 -> x0, starting transfers between devices: 22.1 us -> none  [shifted_2(): return lax.ppermute(value, axis, pairs)]
    all_gather x1 -> x0, waiting for transfers between devices: 21.1 us -> none  [body(): lax.all_gather(rhs_leaf, 'tile', axis=0, tiled=True)]
    another operation x8 -> x0, local copies, waits for them, and re-layouts: 10.9 us -> none
  transfers between devices with their start and end apart: 18 -> 0, of which waited for: 18 -> 0; matrix products, arithmetic and copies ran while one was open for 0% -> 0% of each run, Pallas kernels for 0% -> 0%
where the time goes in v1:
time: 147 us; the launch traced here: 146 us
  Pallas kernels  142 us (97%)
  local copies, waits for them, and re-layouts  3.29 us (2%)
    pallas_call x1, Pallas kernels, body(): pl.pallas_call(functools.partial(kernel, leaves), out_shape=(jax.ShapeDty...  142 us
    unnamed x2, local copies, waits for them, and re-layouts  3.29 us

profile of v1, /device:TPU:0, one launch (start us, length us, event | category | flops | bytes accessed | tf_op | source)
XLA Modules:
  0.0 146.4 jit_solution(2186264391896440748)
XLA Ops:
  0.6 142.5 %shard_map.86 = (f32[512,128]{1,0:T(8,128)}, f32[384,128]{1,0:T(8,128)}) custom-call(s32[8]{0:T(128)} %live_ref.1, f32[512,128]{1,0:T(8,128)} %rhs_leaf.1, f32[384,128]{1,0:T(8,128)} %rhs_sep.1, f32[512,2048]{1,0:T(8,128)} %leaf_inv.1, f32[1536,512]{1,0:T(8,128)} %bitcast.2, f32[384,1536]{1,0:T(8,128)} %sep_inv.1, f32[1536,384]{1,0:T(8,128)} %bitcast.3), custom_call_target="tpu_custom_call" | custom-call | flops 1543503872 | bytes 12582912 | tf_op jit(solution)/shard_map/pallas_call | solution.py:495
  143.1 1.7 %copy.11 = f32[512,128]{1,0:T(8,128)} copy(f32[512,128]{1,0:T(8,128)} %get-tuple-element.4) | data formatting | bytes 524288
  144.8 1.6 %copy.12 = f32[384,128]{1,0:T(8,128)} copy(f32[384,128]{1,0:T(8,128)} %get-tuple-element.5) | data formatting | bytes 393216

commit v2 on v1

v2 whole, which is shorter than its diff:
```python
import functools
import jax
import jax.numpy as jnp
from jax import lax
from jax.experimental import pallas as pl
from jax.experimental.pallas import tpu as pltpu
from jax.sharding import PartitionSpec as P

TILE = 128
PIECES = 2
SKEW = 1
MESH = pl.DeviceIdType.MESH
F32 = jnp.float32
BF16 = jnp.bfloat16

LEAF_GATHER, LEAF_SUM, SEP_GATHER, SEP_SUM = 0, 3, 6, 9
BACK_GATHER, BACK_SUM, LAST_GATHER, LAST_SUM = 12, 15, 18, 21
KID, ABOVE, LEAF_ABOVE, ABOVE_RIGHT = 24, 26, 27, 28
KINDS = 29


def split(value):
    high = value.astype(BF16)
    return high, (value - high.astype(F32)).astype(BF16)


def times(value, high_ref, low_ref, index, transposed):
    dims = (((1,), (1 if transposed else 0,)), ((), ()))
    rows = value.shape[0]
    high, low = split(value)
    both = jnp.concatenate([high, low], axis=0)
    first = lax.dot_general(both, high_ref[index], dims, preferred_element_type=F32)
    second = lax.dot_general(high, low_ref[index], dims, preferred_element_type=F32)
    return first[:rows] + first[rows:] + second


def kernel(
    leaves,
    live_ref,
    rhs_leaf,
    rhs_sep,
    leaf_inv,
    leaf_up,
    sep_inv,
    sep_up,
    leaf_out,
    sep_out,
    rhs_l,
    rhs_s,
    li,
    lu,
    si,
    su,
    li_h,
    li_l,
    lu_h,
    lu_l,
    si_h,
    si_l,
    su_h,
    su_l,
    gather_l,
    gather_s,
    gather_b,
    gather_c,
    part_l,
    part_s,
    part_b,
    part_c,
    one_l,
    one_s,
    one_b,
    one_c,
    two_l,
    two_s,
    two_b,
    two_c,
    kid,
    solved_l,
    solved_s,
    acc_s,
    acc_l,
    load_sem,
    send_sem,
    recv_sem,
):
    depth = leaves.bit_length() - 1
    first_block = leaves // 4 + 1
    leaf = lax.axis_index("leaf")
    t = lax.axis_index("tile")
    core = t % 2
    half = t // 2
    sib = t + 1 - 2 * core
    acr = (t + 2) % 4
    far = (sib + 2) % 4
    pos = (leaf + leaves - first_block) % leaves
    ahead = pos + 1
    share = rhs_s.shape[0]
    cols = rhs_s.shape[1]
    rows = cols // PIECES

    def block_of(place):
        return (place + leaves + first_block) % leaves

    level_one = ahead % 2 == 1
    has_sep = pos < leaves - 1
    is_top = ahead == leaves // 2
    not_top = jnp.logical_and(has_sep, ahead != leaves // 2)
    has_kids = jnp.logical_and(has_sep, ahead % 2 == 0)
    parent = pos * 0
    side = pos * 0
    reach = pos * 0
    for level in range(1, depth + 1):
        own = (ahead % (1 << level) == (1 << (level - 1))).astype(jnp.int32)
        odd = (ahead // (1 << level)) % 2
        step = 1 << (level - 1)
        parent = parent + own * (pos + step - 2 * step * odd)
        side = side + own * odd
        reach = reach + own * (step // 2)
    up_block = block_of(parent)
    left_block = block_of(pos - reach)
    right_block = block_of(pos + reach)
    pair_block = block_of(pos + 1 - 2 * (pos % 2))

    def loads(kind, source, target, by_column):
        out = []
        for q in range(4):
            if by_column:
                width = target.shape[2]
                view = source.at[:, pl.ds(q * width, width)]
            else:
                height = target.shape[1]
                view = source.at[pl.ds(q * height, height), :]
            out.append(pltpu.make_async_copy(view, target.at[q], load_sem.at[kind, q]))
        return out

    load_rl = pltpu.make_async_copy(rhs_leaf, rhs_l, load_sem.at[4, 0])
    load_rs = pltpu.make_async_copy(rhs_sep, rhs_s, load_sem.at[4, 1])
    load_li = loads(0, leaf_inv, li, True)
    load_lu = loads(1, leaf_up, lu, False)
    load_si = loads(2, sep_inv, si, True)
    load_su = loads(3, sep_up, su, False)
    load_rl.start()
    for copy in load_li + load_lu:
        copy.start()
    load_rs.start()
    for copy in load_si + load_su:
        copy.start()

    barrier = pltpu.get_barrier_semaphore()

    def greet(block, tile):
        pl.semaphore_signal(barrier, inc=1, device_id=(block, tile), device_id_type=MESH)

    greet(leaf, sib)
    greet(leaf, acr)
    greet(pair_block, t)

    @pl.when(not_top)
    def _():
        greet(up_block, t)

    @pl.when(has_kids)
    def _():
        greet(left_block, t)
        greet(right_block, t)

    def split_weights(copies, source, high, low):
        for q in range(4):
            copies[q].wait()
            height = source.shape[1]

            def body(i, carry, q=q):
                at = pl.ds(pl.multiple_of(i * 64, 64), 64)
                h, l = split(source[q, at, :])
                high[q, at, :] = h
                low[q, at, :] = l
                return carry

            lax.fori_loop(0, height // 64, body, 0)

    load_rl.wait()
    gather_l[t] = rhs_l[...].T

    pl.semaphore_wait(
        barrier, 3 + not_top.astype(jnp.int32) + 2 * has_kids.astype(jnp.int32)
    )

    pending = []

    def when(conds, run):
        conds = [cond for cond in conds if cond is not None]
        if not conds:
            run()
        else:
            pl.when(conds[0])(lambda: when(conds[1:], run))

    def at(p):
        return pl.ds(p * rows, rows)

    def piece(ref, q, p):
        return lambda: ref.at[at(p)] if q is None else ref.at[q, at(p)]

    def send(kind, p, source, target, block, tile, outer, gate, slot=None):
        def make():
            return pltpu.make_async_remote_copy(
                src_ref=source(),
                dst_ref=target(),
                send_sem=send_sem.at[kind, p],
                recv_sem=recv_sem.at[kind if slot is None else slot, p],
                device_id=(block, tile),
                device_id_type=MESH,
            )

        when(gate, lambda: make().start())
        pending.append((outer + gate, lambda: make().wait_send()))

    def arrive(kind, p, target):
        pltpu.make_async_remote_copy(
            src_ref=target(),
            dst_ref=target(),
            send_sem=send_sem.at[kind, p],
            recv_sem=recv_sem.at[kind, p],
            device_id=(leaf, sib),
            device_id_type=MESH,
        ).wait_recv()

    def run(chain):
        chains = [chain(p) for p in range(PIECES)]
        alive = [True] * PIECES
        turn = 0
        while any(alive):
            for p in range(PIECES):
                if alive[p] and turn >= SKEW * p:
                    alive[p] = next(chains[p], "end") != "end"
            turn += 1

    low_core, high_core = core == 0, core == 1
    low_half, high_half = half == 0, half == 1

    def gather_send(kind, ref, p, triangle, outer, gate):
        mine = piece(ref, t, p)
        send(kind + 1, p, mine, mine, leaf, acr, outer, gate + (low_half if triangle else None,))
        send(kind, p, mine, mine, leaf, sib, outer, gate + (low_core if triangle else None,))

    def gather_use(kind, ref, acc, high, low, triangle, outer, gate, transposed, p):
        cores = gate + (high_core if triangle else None,)
        halves = gate + (high_half if triangle else None,)

        def add(q):
            acc[at(p), :] += times(ref[q, at(p), :], high, low, q, transposed)

        def own():
            acc[at(p), :] = times(ref[t, at(p), :], high, low, t, transposed)

        def from_sib():
            arrive(kind, p, piece(ref, sib, p))
            add(sib)

        def from_far():
            arrive(kind + 2, p, piece(ref, far, p))
            add(far)

        when(gate, own)
        yield
        when(cores, from_sib)
        got = piece(ref, acr, p)
        when(halves, lambda: arrive(kind + 1, p, got))
        send(kind + 2, p, got, got, leaf, sib, outer, halves)
        when(halves, lambda: add(acr))
        yield
        when(halves, from_far)

    def sum_scatter(kind, value, part, one, two, high, low, triangle, outer, gate, transposed, p):
        over = gate + (high_half if triangle else None,)
        giving = gate + (high_core if triangle else None,)
        taking = gate + (low_core if triangle else None,)
        taking_far = gate + (low_half if triangle else None,)

        def work(q):
            part[q, at(p), :] = times(value[at(p), :], high, low, q, transposed)

        when(over, lambda: work(far))
        send(kind, p, piece(part, far, p), piece(one, 0, p), leaf, sib, outer, over)
        when(over, lambda: work(acr))
        when(giving, lambda: work(sib))
        send(kind + 2, p, piece(part, sib, p), piece(one, 1, p), leaf, sib, outer, giving)
        yield

        def pass_on():
            arrive(kind, p, piece(one, 0, p))
            part[acr, at(p), :] += one[0, at(p), :]

        when(over, pass_on)
        send(kind + 1, p, piece(part, acr, p), piece(two, None, p), leaf, acr, outer, over)
        when(gate, lambda: work(t))

        def from_sib():
            arrive(kind + 2, p, piece(one, 1, p))
            part[t, at(p), :] += one[1, at(p), :]

        when(taking, from_sib)
        yield

        def from_acr():
            arrive(kind + 1, p, piece(two, None, p))
            part[t, at(p), :] += two[at(p), :]

        when(taking_far, from_acr)

    is_odd = pos % 2 == 1
    is_even = pos % 2 == 0
    for p in range(PIECES):
        gather_send(LEAF_GATHER, gather_l, p, True, (), ())
    split_weights(load_li, li, li_h, li_l)
    split_weights(load_lu, lu, lu_h, lu_l)

    def leaf_up_chain(p):
        yield from gather_use(
            LEAF_GATHER, gather_l, solved_l, li_h, li_l, True, (), (), True, p
        )
        yield from sum_scatter(
            LEAF_SUM, solved_l, part_l, one_l, two_l, lu_h, lu_l, False, (), (), True, p
        )

        @pl.when(is_even)
        def _():
            kid[0, at(p), :] = part_l[t, at(p), :]

        send(
            KID, p, piece(part_l, t, p), piece(kid, 1, p), pair_block, t, (), (is_odd,), KID + 1
        )

    run(leaf_up_chain)
    split_weights(load_si, si, si_h, si_l)
    split_weights(load_su, su, su_h, su_l)
    load_rs.wait()

    live = live_ref[leaf]
    index = lax.broadcasted_iota(jnp.int32, (1, share), 1) + t * share
    mask = jnp.where(index < live * TILE, 1.0, 0.0).astype(F32)

    @pl.when(has_sep)
    def _():
        inside = (has_sep,)
        linked = (not_top,)
        acc_s[...] = rhs_s[...].T

        def sep_up_chain(p):
            when((has_kids,), lambda: arrive(KID, p, piece(kid, 0, p)))
            arrive(KID + 1, p, piece(kid, 1, p))
            gather_s[t, at(p), :] = (
                acc_s[at(p), :] - kid[0, at(p), :] - kid[1, at(p), :]
            ) * mask
            gather_send(SEP_GATHER, gather_s, p, True, inside, ())
            yield from gather_use(
                SEP_GATHER, gather_s, solved_s, si_h, si_l, True, inside, (), True, p
            )
            solved_s[at(p), :] = solved_s[at(p), :] * mask
            yield from sum_scatter(
                SEP_SUM, solved_s, part_s, one_s, two_s, su_h, su_l, False, inside, linked, True, p
            )

            def make():
                return pltpu.make_async_remote_copy(
                    src_ref=part_s.at[t, at(p)],
                    dst_ref=kid.at[side, at(p)],
                    send_sem=send_sem.at[ABOVE_RIGHT, p],
                    recv_sem=recv_sem.at[KID + side, p],
                    device_id=(up_block, t),
                    device_id_type=MESH,
                )

            when(linked, lambda: make().start())
            pending.append((inside + linked, lambda: make().wait_send()))

        run(sep_up_chain)

        def sep_down_chain(p):
            when(linked, lambda: arrive(ABOVE, p, piece(gather_b, t, p)))
            gather_send(BACK_GATHER, gather_b, p, False, inside, linked)
            yield from gather_use(
                BACK_GATHER, gather_b, acc_s, su_h, su_l, False, inside, linked, False, p
            )

            @pl.when(not_top)
            def _():
                solved_s[at(p), :] = (solved_s[at(p), :] - acc_s[at(p), :]) * mask

            yield from sum_scatter(
                BACK_SUM, solved_s, part_b, one_b, two_b, si_h, si_l, True, inside, (), False, p
            )
            part_b[t, at(p), :] = part_b[t, at(p), :] * mask
            mine = piece(part_b, t, p)
            there = piece(gather_b, t, p)
            here = piece(gather_c, t, p)
            send(ABOVE, p, mine, there, left_block, t, inside, (has_kids,))
            send(ABOVE_RIGHT + 1, p, mine, there, right_block, t, inside, (has_kids,), ABOVE)
            send(LEAF_ABOVE, p, mine, here, pair_block, t, inside, (level_one,))

            @pl.when(level_one)
            def _():
                gather_c[t, at(p), :] = part_b[t, at(p), :]

        run(sep_down_chain)
        sep_out[...] = part_b[t].T

    @pl.when(pos == leaves - 1)
    def _():
        sep_out[...] = jnp.zeros_like(sep_out)

    def leaf_down_chain(p):
        when((is_odd,), lambda: arrive(LEAF_ABOVE, p, piece(gather_c, t, p)))
        gather_send(LAST_GATHER, gather_c, p, False, (), ())
        yield from gather_use(
            LAST_GATHER, gather_c, acc_l, lu_h, lu_l, False, (), (), False, p
        )
        solved_l[at(p), :] = solved_l[at(p), :] - acc_l[at(p), :]
        yield from sum_scatter(
            LAST_SUM, solved_l, part_c, one_c, two_c, li_h, li_l, True, (), (), False, p
        )

    run(leaf_down_chain)
    leaf_out[...] = part_c[t].T
    for conds, wait in pending:
        when(conds, wait)


def body(rhs_leaf, rhs_sep, leaf_inv, leaf_up, sep_inv, sep_up, live_tiles):
    leaves = lax.axis_size("leaf")
    tall, cols = rhs_leaf.shape
    share = rhs_sep.shape[0]
    whole = 4 * share
    any_space = pl.BlockSpec(memory_space=pl.ANY)

    def f32(*shape):
        return pltpu.VMEM(shape, F32)

    weights = [(4, tall, tall), (4, share, tall), (4, share, share), (4, share, share)]
    halves = [pltpu.VMEM(shape, BF16) for shape in weights for _ in range(2)]
    scratch = (
        [f32(tall, cols), f32(share, cols)]
        + [f32(*shape) for shape in weights]
        + halves
        + [f32(4, cols, tall)]
        + [f32(4, cols, share)] * 3
        + [f32(4, cols, share)] * 3
        + [f32(4, cols, tall)]
        + [f32(2, cols, share)] * 3
        + [f32(2, cols, tall)]
        + [f32(cols, share)] * 3
        + [f32(cols, tall)]
        + [f32(2, cols, share), f32(cols, tall), f32(cols, share), f32(cols, share), f32(cols, tall)]
        + [
            pltpu.SemaphoreType.DMA((5, 4)),
            pltpu.SemaphoreType.DMA((KINDS + 1, PIECES)),
            pltpu.SemaphoreType.DMA((KINDS + 1, PIECES)),
        ]
    )
    work = 4 * cols * (tall * 4 * tall + whole * tall + 2 * whole * share)
    return tuple(
        pl.pallas_call(
            functools.partial(kernel, leaves),
            out_shape=(
                jax.ShapeDtypeStruct((tall, cols), F32),
                jax.ShapeDtypeStruct((share, cols), F32),
            ),
            in_specs=[pl.BlockSpec(memory_space=pltpu.SMEM)] + [any_space] * 6,
            out_specs=(
                pl.BlockSpec(memory_space=pltpu.VMEM),
                pl.BlockSpec(memory_space=pltpu.VMEM),
            ),
            scratch_shapes=scratch,
            compiler_params=pltpu.CompilerParams(
                collective_id=0, has_side_effects=True, vmem_limit_bytes=56 * 1024 * 1024
            ),
            cost_estimate=pl.CostEstimate(flops=work, bytes_accessed=12 << 20, transcendentals=0),
        )(live_tiles, rhs_leaf, rhs_sep, leaf_inv, leaf_up[0], sep_inv, sep_up[0])
    )


def solution(mesh):
    return jax.shard_map(
        body,
        mesh=mesh,
        in_specs=(
            P(("leaf", "tile"), None),
            P(("leaf", "tile"), None),
            P(("leaf", "tile"), None),
            P("leaf", None, "tile"),
            P(("leaf", "tile"), None),
            P("leaf", None, "tile"),
            P(),
        ),
        out_specs=(P(("leaf", "tile"), None), P(("leaf", "tile"), None)),
        check_vma=False,
    )
```

time: 147 us -> 133 us (0.905)
  Pallas kernels: 142 us -> 128 us
    pallas_call x1, Pallas kernels: 142 us -> 128 us  [body(): pl.pallas_call(functools.partial(kernel, leaves), out_shape=(jax.ShapeDty...]
where the time goes in v2:
time: 133 us; the launch traced here: 132 us
  Pallas kernels  128 us (96%)
  local copies, waits for them, and re-layouts  3.29 us (2%)
    pallas_call x1, Pallas kernels, body(): pl.pallas_call(functools.partial(kernel, leaves), out_shape=(jax.ShapeDty...  128 us
    unnamed x2, local copies, waits for them, and re-layouts  3.29 us

profile of v2, /device:TPU:0, one launch (start us, length us, event | category | flops | bytes accessed | tf_op | source)
XLA Modules:
  0.0 132.4 jit_solution(14119096647854557826)
XLA Ops:
  0.6 128.5 %shard_map.86 = (f32[512,128]{1,0:T(8,128)}, f32[384,128]{1,0:T(8,128)}) custom-call(s32[8]{0:T(128)} %live_ref.1, f32[512,128]{1,0:T(8,128)} %rhs_leaf.1, f32[384,128]{1,0:T(8,128)} %rhs_sep.1, f32[512,2048]{1,0:T(8,128)} %leaf_inv.1, f32[1536,512]{1,0:T(8,128)} %bitcast.2, f32[384,1536]{1,0:T(8,128)} %sep_inv.1, f32[1536,384]{1,0:T(8,128)} %bitcast.3), custom_call_target="tpu_custom_call" | custom-call | flops 1543503872 | bytes 12582912 | tf_op jit(solution)/shard_map/pallas_call | solution.py:462
  129.1 1.7 %copy.11 = f32[512,128]{1,0:T(8,128)} copy(f32[512,128]{1,0:T(8,128)} %get-tuple-element.4) | data formatting | bytes 524288
  130.8 1.6 %copy.12 = f32[384,128]{1,0:T(8,128)} copy(f32[384,128]{1,0:T(8,128)} %get-tuple-element.5) | data formatting | bytes 393216

commit v3 on v2

--- a/solution.py
+++ b/solution.py
@@ -8,7 +8,7 @@
 
 TILE = 128
 PIECES = 2
-SKEW = 1
+SKEW = 2
 MESH = pl.DeviceIdType.MESH
 F32 = jnp.float32
 BF16 = jnp.bfloat16
@@ -319,9 +319,18 @@
         yield from gather_use(
             LEAF_GATHER, gather_l, solved_l, li_h, li_l, True, (), (), True, p
         )
-        yield from sum_scatter(
+        sums = sum_scatter(
             LEAF_SUM, solved_l, part_l, one_l, two_l, lu_h, lu_l, False, (), (), True, p
         )
+        next(sums)
+        yield
+        next(sums)
+        if p == PIECES - 1:
+            split_weights(load_si, si, si_h, si_l)
+            split_weights(load_su, su, su_h, su_l)
+            load_rs.wait()
+        yield
+        next(sums, None)
 
         @pl.when(is_even)
         def _():
@@ -332,9 +341,6 @@
         )
 
     run(leaf_up_chain)
-    split_weights(load_si, si, si_h, si_l)
-    split_weights(load_su, su, su_h, su_l)
-    load_rs.wait()
 
     live = live_ref[leaf]
     index = lax.broadcasted_iota(jnp.int32, (1, share), 1) + t * share

time: 133 us -> 134 us (level)
  Pallas kernels: 128 us -> 130 us
    pallas_call x1, Pallas kernels: 128 us -> 130 us  [body(): pl.pallas_call(functools.partial(kernel, leaves), out_shape=(jax.ShapeDty...]
where the time goes in v3:
time: 134 us
  Pallas kernels  130 us (97%)
  local copies, waits for them, and re-layouts  3.29 us (2%)
    pallas_call x1, Pallas kernels, body(): pl.pallas_call(functools.partial(kernel, leaves), out_shape=(jax.ShapeDty...  130 us
    unnamed x2, local copies, waits for them, and re-layouts  3.29 us

profile of v3, /device:TPU:0, one launch (start us, length us, event | category | flops | bytes accessed | tf_op | source)
XLA Modules:
  0.0 134.3 jit_solution(11454494914504270767)
XLA Ops:
  0.6 130.4 %shard_map.86 = (f32[512,128]{1,0:T(8,128)}, f32[384,128]{1,0:T(8,128)}) custom-call(s32[8]{0:T(128)} %live_ref.1, f32[512,128]{1,0:T(8,128)} %rhs_leaf.1, f32[384,128]{1,0:T(8,128)} %rhs_sep.1, f32[512,2048]{1,0:T(8,128)} %leaf_inv.1, f32[1536,512]{1,0:T(8,128)} %bitcast.2, f32[384,1536]{1,0:T(8,128)} %sep_inv.1, f32[1536,384]{1,0:T(8,128)} %bitcast.3), custom_call_target="tpu_custom_call" | custom-call | flops 1543503872 | bytes 12582912 | tf_op jit(solution)/shard_map/pallas_call | solution.py:468
  131.0 1.7 %copy.11 = f32[512,128]{1,0:T(8,128)} copy(f32[512,128]{1,0:T(8,128)} %get-tuple-element.4) | data formatting | bytes 524288
  132.7 1.6 %copy.12 = f32[384,128]{1,0:T(8,128)} copy(f32[384,128]{1,0:T(8,128)} %get-tuple-element.5) | data formatting | bytes 393216
